TPU v7x, 256 devices: a whole 4x4x8 slice. The times are simulated.
256 devices in a mesh: sub: 128 (over x_lo, y, z, core), row: 2 (over x_hi).
Axes of the slice: x: 4 (x_hi: 2, x_lo: 2; x = x_hi * 2 + x_lo), y: 4, z: 8, core: 2. Of those that a mesh axis runs over, the one named last changes fastest.
Arguments:
- compliance: bfloat16 [128, 36, 18, 128, 128], P('sub', 'row'), may hold values from -0.0625 to 0.0625
- block_columns: int32 [128, 36, 18], P('sub', 'row'), may hold values from 0 to 35, as said below
- load_response: bfloat16 [128, 32, 4608], P('sub', None, 'row'), may hold values from -6 to 6
- starting_motion: bfloat16 [128, 32, 4608], P('sub', None, 'row'), may hold values from -6 to 6
- start_traction: bfloat16 [128, 32, 4608], P('sub', None, 'row'), may hold values from -6 to 6
- stiffness: float32 [128, 4608], P('sub', 'row'), may hold values from 1 to 10
- history: float32 [128, 4608], P('sub', 'row'), may hold values from 0 to 0.6
- face_partner: int32 [128, 36], P('sub', 'row'), may hold values from -1 to 8, as said below
- orientation: int32 [128, 36, 128], P('sub', 'row'), may hold values from 0 to 127, as said below
Outputs:
- displacement: bfloat16 [128, 32, 4608], P('sub', None, 'row')
- traction: bfloat16 [128, 32, 4608], P('sub', None, 'row')
Inputs may be any that keep to these rules, and one draw needn't show every extreme that they name: `block_columns`: each block row names 18 distinct face columns. `face_partner`: an entry is -1 for a free face, else the position, within the facing group of the same run of the neighbouring substructure, of the matched face. Matches are mutual. Faces facing s+1 on the last substructure and faces facing s-1 on the first are free. In some run of some substructure all 9 faces facing s+1 are matched. `orientation`: each face's row is a permutation of 0 to 127; matched faces carry mutually inverse permutations.
All inputs are finite; a program needn't handle non-finite values.
Results may differ from a plain program's by a relative error of at most 0.0045.
The roundings to bfloat16 on the way count: a program that leaves them out, or rounds other values in their place, can miss the bound.
Values may be sent and summed in bfloat16 or wider, within the bound.
A program may use at most 64 MiB of HBM per device.

v0:
```python
import jax
import jax.numpy as jnp
from jax import lax
from jax.sharding import PartitionSpec as P

SURFACE_EXTENT = 128
ITERS = 3
search_stiffness = 1.0
onset_jump = 0.15
failure_jump = 1.5


def with_halo(cells, sides, width):
    for axis, dim in sides:
        count = lax.axis_size(axis)
        ends = count - 1
        head = lax.slice_in_dim(cells, 0, width, axis=dim)
        tail = lax.slice_in_dim(cells, cells.shape[dim] - width, cells.shape[dim], axis=dim)
        cells = jnp.concatenate(
            [
                lax.ppermute(tail, axis, [(i, (i + 1) % count) for i in range(ends)]),
                cells,
                lax.ppermute(head, axis, [((i + 1) % count, i) for i in range(ends)]),
            ],
            axis=dim,
        )
    return cells


def cohesive(upward_marker, constitutive_parameters, opposing_surface, live_mask):
    temporal_points = upward_marker.shape[0]
    mate_upward_marker = opposing_surface[:temporal_points]
    joint_rigidity = 0.5 * (constitutive_parameters[0] + opposing_surface[temporal_points])
    joint_record = jnp.maximum(constitutive_parameters[1], opposing_surface[temporal_points + 1])
    difference = upward_marker - mate_upward_marker
    jump_size = difference / (search_stiffness + 2.0 * joint_rigidity)
    running_peak = lax.associative_scan(jnp.maximum, jnp.abs(jump_size), axis=0)
    peak_jump = jnp.maximum(joint_record, running_peak)
    damage = jnp.clip((peak_jump - onset_jump) / (failure_jump - onset_jump), 0.0, 1.0)
    effective = joint_rigidity * (1.0 - damage)
    traction = jnp.where(
        live_mask, effective * difference / (search_stiffness + 2.0 * effective), 0.0
    )
    displacement = (traction - upward_marker) / search_stiffness
    return (displacement, traction)


def shards(
    compliance,
    block_columns,
    load_response,
    starting_motion,
    start_traction,
    stiffness,
    history,
    face_partner,
    orientation,
):
    compliance_rows = compliance[0]
    columns = block_columns[0]
    temporal_points = starting_motion.shape[1]
    segment_breadth = starting_motion.shape[2]
    number_surfaces = segment_breadth // SURFACE_EXTENT
    group_size = number_surfaces // 2
    stored_blocks = columns.shape[1]
    applied_forces = load_response[0].astype(jnp.float32)
    constitutive_parameters = jnp.stack([stiffness[0], history[0]]).reshape(
        2, number_surfaces, SURFACE_EXTENT
    )
    partner_table = face_partner[0]
    turning = orientation[0]
    turn_table = (
        turning[:, :, None] == jnp.arange(SURFACE_EXTENT, dtype=jnp.int32)[None, None, :]
    ).astype(jnp.float32)
    facing_up = jnp.arange(number_surfaces) < group_size
    live_mask = (partner_table >= 0)[:, None]
    safe_index = jnp.maximum(partner_table, 0)
    source = jnp.where(facing_up, safe_index, group_size + safe_index)
    present_motion = starting_motion[0].astype(jnp.float32)
    present_stress = start_traction[0].astype(jnp.float32)
    for iteration in range(ITERS):
        robin_sum = present_stress + search_stiffness * present_motion
        gathered_entries = lax.all_gather(robin_sum.astype(jnp.bfloat16), "row", axis=1, tiled=True)
        flexibility_tiles = gathered_entries.reshape(temporal_points, -1, SURFACE_EXTENT)

        def add_block(index, total):
            column_slice = lax.dynamic_index_in_dim(columns, index, 1, keepdims=False)
            piece = jnp.take(flexibility_tiles, column_slice, axis=1)
            block = lax.dynamic_index_in_dim(compliance_rows, index, 1, keepdims=False)
            return total + jnp.einsum(
                "tib,iab->tia", piece, block, preferred_element_type=jnp.float32
            )

        starting_total = jnp.zeros((temporal_points, number_surfaces, SURFACE_EXTENT), jnp.float32)
        operator_multiply = lax.fori_loop(0, stored_blocks, add_block, starting_total)
        proportional_reaction = (
            operator_multiply.reshape(temporal_points, segment_breadth) + applied_forces
        )
        upward_marker = (robin_sum - 2.0 * search_stiffness * proportional_reaction).reshape(
            temporal_points, number_surfaces, SURFACE_EXTENT
        )
        payload = jnp.concatenate([upward_marker, constitutive_parameters], axis=0)[None]
        neighbours = with_halo(payload, (("sub", 0),), 1)
        below_faces = neighbours[0, :, :group_size]
        above_faces = neighbours[2, :, group_size:]
        combined = jnp.concatenate([above_faces, below_faces], axis=1)
        chosen = jnp.take(combined, source, axis=1)
        opposing_surface = jnp.einsum(
            "tfy,fxy->tfx", chosen, turn_table, precision=lax.Precision.HIGHEST
        )
        motion_distribution, stress_distribution = cohesive(
            upward_marker, constitutive_parameters, opposing_surface, live_mask
        )
        present_motion = motion_distribution.reshape(temporal_points, segment_breadth)
        present_stress = stress_distribution.reshape(temporal_points, segment_breadth)
    return (present_motion.astype(jnp.bfloat16)[None], present_stress.astype(jnp.bfloat16)[None])


def solution(mesh):
    in_specs = (
        P("sub", "row", None, None, None),
        P("sub", "row", None),
        P("sub", None, "row"),
        P("sub", None, "row"),
        P("sub", None, "row"),
        P("sub", "row"),
        P("sub", "row"),
        P("sub", "row"),
        P("sub", "row", None),
    )
    out_specs = (P("sub", None, "row"), P("sub", None, "row"))
    return jax.shard_map(shards, mesh=mesh, in_specs=in_specs, out_specs=out_specs, check_vma=False)
```

profile of v0, /device:TPU:6, one launch (start us, length us, event | category | flops | bytes accessed | tf_op | source)
XLA Modules:
  0.0 213.4 jit_solution(7037482593136003585)
XLA Ops:
  1.7 9.7 %copy.62 = bf16[1,18,18,128,128]{4,3,1,2,0:T(8,128)(2,1)} copy(bf16[1,18,18,128,128]{4,3,2,1,0:T(8,128)(2,1)} %param.19) | data formatting | bytes 21233664 | tf_op args[0]
  11.5 7.7 %all-gather = bf16[1,32,4608]{2,1,0:T(8,128)(2,1)S(1)} all-gather(bf16[1,32,2304]{2,1,0:T(8,128)(2,1)S(1)} %get-tuple-element.411), channel_id=2, replica_groups=mesh['sub'=128,'row'=2] {'row'}, dimensions={2}, use_global_device_ids=true | all-gather | bytes 442368 | tf_op jit(solution)/shard_map/all_gather | solution.py:83
  19.5 38.6 %while.42 = (s32[]{:T(128)}, f32[32,18,128]{2,0,1:T(8,128)S(1)}, bf16[18,18,128,128]{3,2,0,1:T(8,128)(2,1)}, s32[18,18]{0,1:T(8,128)S(1)}, bf16[32,36,128]{2,0,1:T(8,128)(2,1)S(1)}, /*index=5*/s32[]{:T(128)}, s32[]{:T(128)}) while((s32[]{:T(128)}, f32[32,18,128]{2,0,1:T(8,128)S(1)}, bf16[18,18,128,128]{3,2,0,1:T(8,128)(2,1)}, ...), condition=%wide.region_1.0_spmd.clone, body=%wide.region_0.2_spmd.clone.sunk | while | flops 19096688 | bytes 1626539 | solution.py:95
  22.3 1.5 fusion.72
  58.5 1.9 collective-permute-start.1
  60.4 9.1 %collective-permute-start = (f32[1,34,18,128]{3,1,2,0:T(8,128)S(1)}, f32[1,34,18,128]{3,1,2,0:T(8,128)S(1)}, u32[]{:S(2)}, u32[]{:S(2)}) collective-permute-start(f32[1,34,18,128]{3,1,2,0:T(8,128)S(1)} %fusion.30), channel_id=1, source_target_pairs={{2,0},{4,2},{6,4},{8,6},{10,8},{12,10},{14,12},{16,14},{18,16},{20... | collective-permute-start | bytes 940040 | tf_op jit(solution)/shard_map/ppermute | solution.py:23
  69.6 3.2 %collective-permute-done.1 = f32[1,34,18,128]{3,1,2,0:T(8,128)S(1)} collective-permute-done((f32[1,34,18,128]{3,1,2,0:T(8,128)S(1)}, f32[1,34,18,128]{3,1,2,0:T(8,128)S(1)}, u32[]{:S(2)}, u32[]{:S(2)}) %collective-permute-start.1) | collective-permute-done | bytes 313376 | tf_op jit(solution)/shard_map/ppermute | solution.py:21
  72.7 1.7 collective-permute-done
  75.1 1.7 convolution_bitcast_fusion.5
  79.6 7.3 %all_gather.10 = bf16[32,4608]{1,0:T(8,128)(2,1)S(1)} all-gather(bf16[32,2304]{1,0:T(8,128)(2,1)S(1)} %bitcast.172), channel_id=1, replica_groups=mesh['sub'=128,'row'=2] {'row'}, dimensions={1}, use_global_device_ids=true | all-gather | bytes 442368 | tf_op jit(solution)/shard_map/all_gather | solution.py:83
  86.9 38.6 %while.43 = (s32[]{:T(128)}, f32[32,18,128]{2,0,1:T(8,128)S(1)}, bf16[18,18,128,128]{3,2,0,1:T(8,128)(2,1)}, s32[18,18]{0,1:T(8,128)S(1)}, bf16[32,36,128]{2,0,1:T(8,128)(2,1)S(1)}, /*index=5*/s32[]{:T(128)}, s32[]{:T(128)}) while((s32[]{:T(128)}, f32[32,18,128]{2,0,1:T(8,128)S(1)}, bf16[18,18,128,128]{3,2,0,1:T(8,128)(2,1)}, ...), condition=%wide.region_3.6_spmd.clone, body=%wide.region_2.5_spmd.clone.sunk | while | flops 19096688 | bytes 1626539 | solution.py:95
  102.6 1.5 fusion.75
  125.8 1.9 collective-permute-start.3
  127.7 7.9 %collective-permute-start.2 = (f32[1,34,18,128]{3,1,2,0:T(8,128)S(1)}, f32[1,34,18,128]{3,1,2,0:T(8,128)S(1)}, u32[]{:S(2)}, u32[]{:S(2)}) collective-permute-start(f32[1,34,18,128]{3,1,2,0:T(8,128)S(1)} %fusion.31), channel_id=1, source_target_pairs={{2,0},{4,2},{6,4},{8,6},{10,8},{12,10},{14,12},{16,14},{18,16},{20... | collective-permute-start | bytes 940040 | tf_op jit(solution)/shard_map/ppermute | solution.py:23
  135.6 3.2 %collective-permute-done.3 = f32[1,34,18,128]{3,1,2,0:T(8,128)S(1)} collective-permute-done((f32[1,34,18,128]{3,1,2,0:T(8,128)S(1)}, f32[1,34,18,128]{3,1,2,0:T(8,128)S(1)}, u32[]{:S(2)}, u32[]{:S(2)}) %collective-permute-start.3) | collective-permute-done | bytes 313376 | tf_op jit(solution)/shard_map/ppermute | solution.py:21
  138.8 1.7 collective-permute-done.2
  141.2 1.7 convolution_bitcast_fusion.4
  145.7 7.3 %all_gather.11 = bf16[32,4608]{1,0:T(8,128)(2,1)S(1)} all-gather(bf16[32,2304]{1,0:T(8,128)(2,1)S(1)} %bitcast.173), channel_id=1, replica_groups=mesh['sub'=128,'row'=2] {'row'}, dimensions={1}, use_global_device_ids=true | all-gather | bytes 442368 | tf_op jit(solution)/shard_map/all_gather | solution.py:83
  153.0 38.6 %while.44 = (s32[]{:T(128)}, f32[32,18,128]{2,0,1:T(8,128)S(1)}, bf16[18,18,128,128]{3,2,0,1:T(8,128)(2,1)}, s32[18,18]{0,1:T(8,128)S(1)}, bf16[32,36,128]{2,0,1:T(8,128)(2,1)S(1)}, /*index=5*/s32[]{:T(128)}, s32[]{:T(128)}) while((s32[]{:T(128)}, f32[32,18,128]{2,0,1:T(8,128)S(1)}, bf16[18,18,128,128]{3,2,0,1:T(8,128)(2,1)}, ...), condition=%wide.region_5.8_spmd.clone, body=%wide.region_4.7_spmd.clone.sunk | while | flops 19096688 | bytes 1626539 | solution.py:95
  191.8 1.9 collective-permute-start.5
  193.8 7.9 %collective-permute-start.4 = (f32[1,34,18,128]{3,1,2,0:T(8,128)S(1)}, f32[1,34,18,128]{3,1,2,0:T(8,128)S(1)}, u32[]{:S(2)}, u32[]{:S(2)}) collective-permute-start(f32[1,34,18,128]{3,1,2,0:T(8,128)S(1)} %fusion.32), channel_id=1, source_target_pairs={{2,0},{4,2},{6,4},{8,6},{10,8},{12,10},{14,12},{16,14},{18,16},{20... | collective-permute-start | bytes 940040 | tf_op jit(solution)/shard_map/ppermute | solution.py:23
  201.6 3.3 %collective-permute-done.5 = f32[1,34,18,128]{3,1,2,0:T(8,128)S(1)} collective-permute-done((f32[1,34,18,128]{3,1,2,0:T(8,128)S(1)}, f32[1,34,18,128]{3,1,2,0:T(8,128)S(1)}, u32[]{:S(2)}, u32[]{:S(2)}) %collective-permute-start.5) | collective-permute-done | bytes 313376 | tf_op jit(solution)/shard_map/ppermute | solution.py:21
  204.9 1.7 collective-permute-done.4
  207.3 1.7 convolution_bitcast_fusion.3
  (401 shorter events, 124.2 us)
Async XLA Ops:
  1.7 9.7 %copy-start.3 = (s32[1,18,18]{2,0,1:T(1,128)S(1)}, s32[1,18,18]{2,0,1:T(1,128)}, u32[]{:S(2)}) copy-start(s32[1,18,18]{2,0,1:T(1,128)} %param.20) | copy-start | bytes 3892
  1.7 56.4 %copy-start = (bf16[1,32,2304]{2,1,0:T(8,128)(2,1)S(1)}, bf16[1,32,2304]{2,1,0:T(8,128)(2,1)}, u32[]{:S(2)}) copy-start(bf16[1,32,2304]{2,1,0:T(8,128)(2,1)} %param.21) | copy-start | bytes 442372
  11.4 46.8 %copy-start.1 = (f32[1,2304]{1,0:T(1,128)S(1)}, f32[1,2304]{1,0:T(1,128)}, u32[]{:S(2)}) copy-start(f32[1,2304]{1,0:T(1,128)} %param.25) | copy-start | bytes 27652
  11.4 46.9 %copy-start.2 = (f32[1,2304]{1,0:T(1,128)S(1)}, f32[1,2304]{1,0:T(1,128)}, u32[]{:S(2)}) copy-start(f32[1,2304]{1,0:T(1,128)} %param.24) | copy-start | bytes 27652
  11.4 58.1 %copy-start.4 = (s32[1,18,128]{2,0,1:T(1,128)S(1)}, s32[1,18,128]{2,0,1:T(1,128)}, u32[]{:S(2)}) copy-start(s32[1,18,128]{2,0,1:T(1,128)} %param.27) | copy-start | bytes 27652
  11.4 58.1 %copy-start.5 = (s32[1,18]{1,0:T(1,128)S(1)}, s32[1,18]{1,0:T(1,128)}, u32[]{:S(2)}) copy-start(s32[1,18]{1,0:T(1,128)} %param.26) | copy-start | bytes 220
  58.5 14.2 %collective-permute-start.1 = (f32[1,34,18,128]{3,1,2,0:T(8,128)S(1)}, f32[1,34,18,128]{3,1,2,0:T(8,128)S(1)}, u32[]{:S(2)}, u32[]{:S(2)}) collective-permute-start(f32[1,34,18,128]{3,1,2,0:T(8,128)S(1)} %fusion.30), channel_id=1, source_target_pairs={{0,2},{2,4},{4,6},{6,8},{8,10},{10,12},{12,14},{14,16},{16,18},{18... | collective-permute-start | bytes 940040 | tf_op jit(solution)/shard_map/ppermute | solution.py:21
  60.4 14.1 %collective-permute-start = (f32[1,34,18,128]{3,1,2,0:T(8,128)S(1)}, f32[1,34,18,128]{3,1,2,0:T(8,128)S(1)}, u32[]{:S(2)}, u32[]{:S(2)}) collective-permute-start(f32[1,34,18,128]{3,1,2,0:T(8,128)S(1)} %fusion.30), channel_id=1, source_target_pairs={{2,0},{4,2},{6,4},{8,6},{10,8},{12,10},{14,12},{16,14},{18,16},{20... | collective-permute-start | bytes 940040 | tf_op jit(solution)/shard_map/ppermute | solution.py:23
  125.8 13.1 %collective-permute-start.3 = (f32[1,34,18,128]{3,1,2,0:T(8,128)S(1)}, f32[1,34,18,128]{3,1,2,0:T(8,128)S(1)}, u32[]{:S(2)}, u32[]{:S(2)}) collective-permute-start(f32[1,34,18,128]{3,1,2,0:T(8,128)S(1)} %fusion.31), channel_id=1, source_target_pairs={{0,2},{2,4},{4,6},{6,8},{8,10},{10,12},{12,14},{14,16},{16,18},{18... | collective-permute-start | bytes 940040 | tf_op jit(solution)/shard_map/ppermute | solution.py:21
  127.7 12.9 %collective-permute-start.2 = (f32[1,34,18,128]{3,1,2,0:T(8,128)S(1)}, f32[1,34,18,128]{3,1,2,0:T(8,128)S(1)}, u32[]{:S(2)}, u32[]{:S(2)}) collective-permute-start(f32[1,34,18,128]{3,1,2,0:T(8,128)S(1)} %fusion.31), channel_id=1, source_target_pairs={{2,0},{4,2},{6,4},{8,6},{10,8},{12,10},{14,12},{16,14},{18,16},{20... | collective-permute-start | bytes 940040 | tf_op jit(solution)/shard_map/ppermute | solution.py:23
  191.8 13.1 %collective-permute-start.5 = (f32[1,34,18,128]{3,1,2,0:T(8,128)S(1)}, f32[1,34,18,128]{3,1,2,0:T(8,128)S(1)}, u32[]{:S(2)}, u32[]{:S(2)}) collective-permute-start(f32[1,34,18,128]{3,1,2,0:T(8,128)S(1)} %fusion.32), channel_id=1, source_target_pairs={{0,2},{2,4},{4,6},{6,8},{8,10},{10,12},{12,14},{14,16},{16,18},{18... | collective-permute-start | bytes 940040 | tf_op jit(solution)/shard_map/ppermute | solution.py:21
  193.8 12.9 %collective-permute-start.4 = (f32[1,34,18,128]{3,1,2,0:T(8,128)S(1)}, f32[1,34,18,128]{3,1,2,0:T(8,128)S(1)}, u32[]{:S(2)}, u32[]{:S(2)}) collective-permute-start(f32[1,34,18,128]{3,1,2,0:T(8,128)S(1)} %fusion.32), channel_id=1, source_target_pairs={{2,0},{4,2},{6,4},{8,6},{10,8},{12,10},{14,12},{16,14},{18,16},{20... | collective-permute-start | bytes 940040 | tf_op jit(solution)/shard_map/ppermute | solution.py:23
where the time goes:
time: 216 us; the launch traced here: 213 us
  matrix products  87.2 us (40%)
  local copies, waits for them, and re-layouts  50.4 us (23%)
  starting transfers between devices  30.5 us (14%)
  blocking collectives  22.4 us (10%)
  waiting for transfers between devices  14.9 us (7%)
  other arithmetic  4.5 us (2%)
    dot_general x54, matrix products, add_block(): jnp.einsum('tib,iab->tia', piece, block, preferred_element_type=jnp.float32)  82 us
    gather x54, local copies, waits for them, and re-layouts, add_block(): piece = jnp.take(flexibility_tiles, column_slice, axis=1)  31 us
    ppermute x3, starting transfers between devices, with_halo(): lax.ppermute(head, axis, [((i + 1) % count, i) for i in range(ends)])  24.8 us
    all_gather x3, blocking collectives, shards(): lax.all_gather(robin_sum.astype(jnp.bfloat16), 'row', axis=1, tiled=True)  22.4 us
    unnamed x26, local copies, waits for them, and re-layouts  9.97 us
    ppermute x3, waiting for transfers between devices, with_halo(): lax.ppermute(tail, axis, [(i, (i + 1) % count) for i in range(ends)])  9.67 us
    ppermute x3, starting transfers between devices, with_halo(): lax.ppermute(tail, axis, [(i, (i + 1) % count) for i in range(ends)])  5.76 us
    ppermute x3, waiting for transfers between devices, with_halo(): lax.ppermute(head, axis, [((i + 1) % count, i) for i in range(ends)])  5.22 us
  transfers between devices with their start and end apart: 6, of which 6 were waited for; matrix products, arithmetic and copies ran while one was open for 0% of the time, Pallas kernels for 0%

commit v1 on v0

--- a/solution.py
+++ b/solution.py
@@ -80,7 +80,12 @@
     present_stress = start_traction[0].astype(jnp.float32)
     for iteration in range(ITERS):
         robin_sum = present_stress + search_stiffness * present_motion
-        gathered_entries = lax.all_gather(robin_sum.astype(jnp.bfloat16), "row", axis=1, tiled=True)
+        gathered_entries = jnp.concatenate(
+            lax.all_to_all(
+                jnp.stack([robin_sum.astype(jnp.bfloat16)] * lax.axis_size("row")), "row", 0, 0
+            ),
+            axis=1,
+        )
         flexibility_tiles = gathered_entries.reshape(temporal_points, -1, SURFACE_EXTENT)
 
         def add_block(index, total):

time: 216 us -> 224 us (1.037)
  the two profiles are of different devices: /device:TPU:6 before, /device:TPU:2 now
where the time goes in v1:
time: 224 us; the launch traced here: 221 us
  matrix products  87.2 us (39%)
  local copies, waits for them, and re-layouts  52 us (23%)
  starting transfers between devices  42.5 us (19%)
  waiting for transfers between devices  28.6 us (13%)
  other arithmetic  7.37 us (3%)
    dot_general x54, matrix products, add_block(): jnp.einsum('tib,iab->tia', piece, block, preferred_element_type=jnp.float32)  82 us
    gather x54, local copies, waits for them, and re-layouts, add_block(): piece = jnp.take(flexibility_tiles, column_slice, axis=1)  31 us
    ppermute x3, starting transfers between devices, with_halo(): lax.ppermute(head, axis, [((i + 1) % count, i) for i in range(ends)])  25.9 us
    all_to_all x3, waiting for transfers between devices, shards(): lax.all_to_all(jnp.stack([robin_sum.astype(jnp.bfloat16)] * lax.axis_size...  13.7 us
    all_to_all x3, starting transfers between devices, shards(): lax.all_to_all(jnp.stack([robin_sum.astype(jnp.bfloat16)] * lax.axis_size...  10.8 us
    unnamed x26, local copies, waits for them, and re-layouts  9.97 us
    ppermute x3, waiting for transfers between devices, with_halo(): lax.ppermute(tail, axis, [(i, (i + 1) % count) for i in range(ends)])  9.72 us
    ppermute x3, starting transfers between devices, with_halo(): lax.ppermute(tail, axis, [(i, (i + 1) % count) for i in range(ends)])  5.76 us
  transfers between devices with their start and end apart: 9, of which 8 were waited for; matrix products, arithmetic and copies ran while one was open for 5% of the time, Pallas kernels for 0%

profile of v1, /device:TPU:2, one launch (start us, length us, event | category | flops | bytes accessed | tf_op | source)
XLA Modules:
  0.0 221.2 jit_solution(10012757225502162354)
XLA Ops:
  2.4 3.4 %all-to-all-start = ((bf16[2,32,2304]{2,1,0:T(8,128)(2,1)}), bf16[2,32,2304]{2,1,0:T(8,128)(2,1)S(1)}, u32[]{:S(2)}, u32[]{:S(2)}) async-start(bf16[2,32,2304]{2,1,0:T(8,128)(2,1)} %pad_maximum_fusion.6), calls=%async_computation | async-start | bytes 589824 | tf_op jit(solution)/shard_map/all_to_all | solution.py:84
  6.6 9.7 %copy.58 = bf16[1,18,18,128,128]{4,3,1,2,0:T(8,128)(2,1)} copy(bf16[1,18,18,128,128]{4,3,2,1,0:T(8,128)(2,1)} %param.19) | data formatting | bytes 21233664 | tf_op args[0]
  17.1 38.6 %while.42 = (s32[]{:T(128)}, f32[32,18,128]{2,0,1:T(8,128)S(1)}, bf16[18,18,128,128]{3,2,0,1:T(8,128)(2,1)}, s32[18,18]{0,1:T(8,128)S(1)}, bf16[32,36,128]{2,0,1:T(8,128)(2,1)S(1)}, /*index=5*/s32[]{:T(128)}, s32[]{:T(128)}) while((s32[]{:T(128)}, f32[32,18,128]{2,0,1:T(8,128)S(1)}, bf16[18,18,128,128]{3,2,0,1:T(8,128)(2,1)}, ...), condition=%wide.region_1.0_spmd.clone, body=%wide.region_0.2_spmd.clone.sunk | while | flops 19096688 | bytes 1626539 | solution.py:100
  56.0 1.9 collective-permute-start.1
  57.9 10.2 %collective-permute-start = (f32[1,34,18,128]{3,1,2,0:T(8,128)S(1)}, f32[1,34,18,128]{3,1,2,0:T(8,128)S(1)}, u32[]{:S(2)}, u32[]{:S(2)}) collective-permute-start(f32[1,34,18,128]{3,1,2,0:T(8,128)S(1)} %fusion.30), channel_id=1, source_target_pairs={{2,0},{4,2},{6,4},{8,6},{10,8},{12,10},{14,12},{16,14},{18,16},{20... | collective-permute-start | bytes 940040 | tf_op jit(solution)/shard_map/ppermute | solution.py:23
  68.1 3.2 %collective-permute-done.1 = f32[1,34,18,128]{3,1,2,0:T(8,128)S(1)} collective-permute-done((f32[1,34,18,128]{3,1,2,0:T(8,128)S(1)}, f32[1,34,18,128]{3,1,2,0:T(8,128)S(1)}, u32[]{:S(2)}, u32[]{:S(2)}) %collective-permute-start.1) | collective-permute-done | bytes 313376 | tf_op jit(solution)/shard_map/ppermute | solution.py:21
  71.4 1.8 collective-permute-done
  73.7 1.7 convolution_bitcast_fusion.5
  79.1 3.9 %all-to-all-start.1 = ((bf16[2,32,2304]{2,1,0:T(8,128)(2,1)}), bf16[2,32,2304]{2,1,0:T(8,128)(2,1)S(1)}, u32[]{:S(2)}, u32[]{:S(2)}) async-start(bf16[2,32,2304]{2,1,0:T(8,128)(2,1)} %pad_maximum_fusion.7), calls=%async_computation.1 | async-start | bytes 589824 | tf_op jit(solution)/shard_map/all_to_all | solution.py:84
  83.0 6.9 %all-to-all-done.1 = bf16[2,32,2304]{2,1,0:T(8,128)(2,1)S(1)} async-done(((bf16[2,32,2304]{2,1,0:T(8,128)(2,1)}), bf16[2,32,2304]{2,1,0:T(8,128)(2,1)S(1)}, u32[]{:S(2)}, u32[]{:S(2)}) %all-to-all-start.1) | async-done | bytes 294944 | tf_op jit(solution)/shard_map/all_to_all | solution.py:84
  90.4 38.6 %while.43 = (s32[]{:T(128)}, f32[32,18,128]{2,0,1:T(8,128)S(1)}, bf16[18,18,128,128]{3,2,0,1:T(8,128)(2,1)}, s32[18,18]{0,1:T(8,128)S(1)}, bf16[32,36,128]{2,0,1:T(8,128)(2,1)S(1)}, /*index=5*/s32[]{:T(128)}, s32[]{:T(128)}) while((s32[]{:T(128)}, f32[32,18,128]{2,0,1:T(8,128)S(1)}, bf16[18,18,128,128]{3,2,0,1:T(8,128)(2,1)}, ...), condition=%wide.region_3.6_spmd.clone, body=%wide.region_2.5_spmd.clone.sunk | while | flops 19096688 | bytes 1626539 | solution.py:100
  129.2 1.9 collective-permute-start.3
  131.1 7.9 %collective-permute-start.2 = (f32[1,34,18,128]{3,1,2,0:T(8,128)S(1)}, f32[1,34,18,128]{3,1,2,0:T(8,128)S(1)}, u32[]{:S(2)}, u32[]{:S(2)}) collective-permute-start(f32[1,34,18,128]{3,1,2,0:T(8,128)S(1)} %fusion.31), channel_id=1, source_target_pairs={{2,0},{4,2},{6,4},{8,6},{10,8},{12,10},{14,12},{16,14},{18,16},{20... | collective-permute-start | bytes 940040 | tf_op jit(solution)/shard_map/ppermute | solution.py:23
  139.0 3.3 %collective-permute-done.3 = f32[1,34,18,128]{3,1,2,0:T(8,128)S(1)} collective-permute-done((f32[1,34,18,128]{3,1,2,0:T(8,128)S(1)}, f32[1,34,18,128]{3,1,2,0:T(8,128)S(1)}, u32[]{:S(2)}, u32[]{:S(2)}) %collective-permute-start.3) | collective-permute-done | bytes 313376 | tf_op jit(solution)/shard_map/ppermute | solution.py:21
  142.3 1.7 collective-permute-done.2
  144.6 1.7 convolution_bitcast_fusion.4
  150.0 3.4 %all-to-all-start.2 = ((bf16[2,32,2304]{2,1,0:T(8,128)(2,1)}), bf16[2,32,2304]{2,1,0:T(8,128)(2,1)S(1)}, u32[]{:S(2)}, u32[]{:S(2)}) async-start(bf16[2,32,2304]{2,1,0:T(8,128)(2,1)} %pad_maximum_fusion.8), calls=%async_computation.2 | async-start | bytes 589824 | tf_op jit(solution)/shard_map/all_to_all | solution.py:84
  153.4 6.8 %all-to-all-done.2 = bf16[2,32,2304]{2,1,0:T(8,128)(2,1)S(1)} async-done(((bf16[2,32,2304]{2,1,0:T(8,128)(2,1)}), bf16[2,32,2304]{2,1,0:T(8,128)(2,1)S(1)}, u32[]{:S(2)}, u32[]{:S(2)}) %all-to-all-start.2) | async-done | bytes 294944 | tf_op jit(solution)/shard_map/all_to_all | solution.py:84
  160.8 38.6 %while.44 = (s32[]{:T(128)}, f32[32,18,128]{2,0,1:T(8,128)S(1)}, bf16[18,18,128,128]{3,2,0,1:T(8,128)(2,1)}, s32[18,18]{0,1:T(8,128)S(1)}, bf16[32,36,128]{2,0,1:T(8,128)(2,1)S(1)}, /*index=5*/s32[]{:T(128)}, s32[]{:T(128)}) while((s32[]{:T(128)}, f32[32,18,128]{2,0,1:T(8,128)S(1)}, bf16[18,18,128,128]{3,2,0,1:T(8,128)(2,1)}, ...), condition=%wide.region_5.8_spmd.clone, body=%wide.region_4.7_spmd.clone.sunk | while | flops 19096688 | bytes 1626539 | solution.py:100
  199.6 1.9 collective-permute-start.5
  201.6 7.9 %collective-permute-start.4 = (f32[1,34,18,128]{3,1,2,0:T(8,128)S(1)}, f32[1,34,18,128]{3,1,2,0:T(8,128)S(1)}, u32[]{:S(2)}, u32[]{:S(2)}) collective-permute-start(f32[1,34,18,128]{3,1,2,0:T(8,128)S(1)} %fusion.32), channel_id=1, source_target_pairs={{2,0},{4,2},{6,4},{8,6},{10,8},{12,10},{14,12},{16,14},{18,16},{20... | collective-permute-start | bytes 940040 | tf_op jit(solution)/shard_map/ppermute | solution.py:23
  209.4 3.3 %collective-permute-done.5 = f32[1,34,18,128]{3,1,2,0:T(8,128)S(1)} collective-permute-done((f32[1,34,18,128]{3,1,2,0:T(8,128)S(1)}, f32[1,34,18,128]{3,1,2,0:T(8,128)S(1)}, u32[]{:S(2)}, u32[]{:S(2)}) %collective-permute-start.5) | collective-permute-done | bytes 313376 | tf_op jit(solution)/shard_map/ppermute | solution.py:21
  212.7 1.7 collective-permute-done.4
  215.1 1.7 convolution_bitcast_fusion.3
  (414 shorter events, 131.6 us)
Async XLA Ops:
  2.4 14.2 %all-to-all-start = ((bf16[2,32,2304]{2,1,0:T(8,128)(2,1)}), bf16[2,32,2304]{2,1,0:T(8,128)(2,1)S(1)}, u32[]{:S(2)}, u32[]{:S(2)}) async-start(bf16[2,32,2304]{2,1,0:T(8,128)(2,1)} %pad_maximum_fusion.6), calls=%async_computation | async-start | bytes 589824 | tf_op jit(solution)/shard_map/all_to_all | solution.py:84
  6.6 9.8 %copy-start.3 = (s32[1,18,18]{2,0,1:T(1,128)S(1)}, s32[1,18,18]{2,0,1:T(1,128)}, u32[]{:S(2)}) copy-start(s32[1,18,18]{2,0,1:T(1,128)} %param.20) | copy-start | bytes 3892
  6.6 9.8 %copy-start = (bf16[1,32,2304]{2,1,0:T(8,128)(2,1)S(1)}, bf16[1,32,2304]{2,1,0:T(8,128)(2,1)}, u32[]{:S(2)}) copy-start(bf16[1,32,2304]{2,1,0:T(8,128)(2,1)} %param.21) | copy-start | bytes 442372
  6.6 9.9 %copy-start.4 = (s32[1,18,128]{2,0,1:T(1,128)S(1)}, s32[1,18,128]{2,0,1:T(1,128)}, u32[]{:S(2)}) copy-start(s32[1,18,128]{2,0,1:T(1,128)} %param.27) | copy-start | bytes 27652
  6.6 9.9 %copy-start.1 = (f32[1,2304]{1,0:T(1,128)S(1)}, f32[1,2304]{1,0:T(1,128)}, u32[]{:S(2)}) copy-start(f32[1,2304]{1,0:T(1,128)} %param.25) | copy-start | bytes 27652
  6.6 9.9 %copy-start.2 = (f32[1,2304]{1,0:T(1,128)S(1)}, f32[1,2304]{1,0:T(1,128)}, u32[]{:S(2)}) copy-start(f32[1,2304]{1,0:T(1,128)} %param.24) | copy-start | bytes 27652
  16.3 41.6 %copy-start.5 = (s32[1,18]{1,0:T(1,128)S(1)}, s32[1,18]{1,0:T(1,128)}, u32[]{:S(2)}) copy-start(s32[1,18]{1,0:T(1,128)} %param.26) | copy-start | bytes 220
  56.0 15.4 %collective-permute-start.1 = (f32[1,34,18,128]{3,1,2,0:T(8,128)S(1)}, f32[1,34,18,128]{3,1,2,0:T(8,128)S(1)}, u32[]{:S(2)}, u32[]{:S(2)}) collective-permute-start(f32[1,34,18,128]{3,1,2,0:T(8,128)S(1)} %fusion.30), channel_id=1, source_target_pairs={{0,2},{2,4},{4,6},{6,8},{8,10},{10,12},{12,14},{14,16},{16,18},{18... | collective-permute-start | bytes 940040 | tf_op jit(solution)/shard_map/ppermute | solution.py:21
  57.9 15.2 %collective-permute-start = (f32[1,34,18,128]{3,1,2,0:T(8,128)S(1)}, f32[1,34,18,128]{3,1,2,0:T(8,128)S(1)}, u32[]{:S(2)}, u32[]{:S(2)}) collective-permute-start(f32[1,34,18,128]{3,1,2,0:T(8,128)S(1)} %fusion.30), channel_id=1, source_target_pairs={{2,0},{4,2},{6,4},{8,6},{10,8},{12,10},{14,12},{16,14},{18,16},{20... | collective-permute-start | bytes 940040 | tf_op jit(solution)/shard_map/ppermute | solution.py:23
  79.1 10.8 %all-to-all-start.1 = ((bf16[2,32,2304]{2,1,0:T(8,128)(2,1)}), bf16[2,32,2304]{2,1,0:T(8,128)(2,1)S(1)}, u32[]{:S(2)}, u32[]{:S(2)}) async-start(bf16[2,32,2304]{2,1,0:T(8,128)(2,1)} %pad_maximum_fusion.7), calls=%async_computation.1 | async-start | bytes 589824 | tf_op jit(solution)/shard_map/all_to_all | solution.py:84
  129.2 13.1 %collective-permute-start.3 = (f32[1,34,18,128]{3,1,2,0:T(8,128)S(1)}, f32[1,34,18,128]{3,1,2,0:T(8,128)S(1)}, u32[]{:S(2)}, u32[]{:S(2)}) collective-permute-start(f32[1,34,18,128]{3,1,2,0:T(8,128)S(1)} %fusion.31), channel_id=1, source_target_pairs={{0,2},{2,4},{4,6},{6,8},{8,10},{10,12},{12,14},{14,16},{16,18},{18... | collective-permute-start | bytes 940040 | tf_op jit(solution)/shard_map/ppermute | solution.py:21
  131.1 12.9 %collective-permute-start.2 = (f32[1,34,18,128]{3,1,2,0:T(8,128)S(1)}, f32[1,34,18,128]{3,1,2,0:T(8,128)S(1)}, u32[]{:S(2)}, u32[]{:S(2)}) collective-permute-start(f32[1,34,18,128]{3,1,2,0:T(8,128)S(1)} %fusion.31), channel_id=1, source_target_pairs={{2,0},{4,2},{6,4},{8,6},{10,8},{12,10},{14,12},{16,14},{18,16},{20... | collective-permute-start | bytes 940040 | tf_op jit(solution)/shard_map/ppermute | solution.py:23
  150.0 10.3 %all-to-all-start.2 = ((bf16[2,32,2304]{2,1,0:T(8,128)(2,1)}), bf16[2,32,2304]{2,1,0:T(8,128)(2,1)S(1)}, u32[]{:S(2)}, u32[]{:S(2)}) async-start(bf16[2,32,2304]{2,1,0:T(8,128)(2,1)} %pad_maximum_fusion.8), calls=%async_computation.2 | async-start | bytes 589824 | tf_op jit(solution)/shard_map/all_to_all | solution.py:84
  199.6 13.1 %collective-permute-start.5 = (f32[1,34,18,128]{3,1,2,0:T(8,128)S(1)}, f32[1,34,18,128]{3,1,2,0:T(8,128)S(1)}, u32[]{:S(2)}, u32[]{:S(2)}) collective-permute-start(f32[1,34,18,128]{3,1,2,0:T(8,128)S(1)} %fusion.32), channel_id=1, source_target_pairs={{0,2},{2,4},{4,6},{6,8},{8,10},{10,12},{12,14},{14,16},{16,18},{18... | collective-permute-start | bytes 940040 | tf_op jit(solution)/shard_map/ppermute | solution.py:21
  201.6 12.9 %collective-permute-start.4 = (f32[1,34,18,128]{3,1,2,0:T(8,128)S(1)}, f32[1,34,18,128]{3,1,2,0:T(8,128)S(1)}, u32[]{:S(2)}, u32[]{:S(2)}) collective-permute-start(f32[1,34,18,128]{3,1,2,0:T(8,128)S(1)} %fusion.32), channel_id=1, source_target_pairs={{2,0},{4,2},{6,4},{8,6},{10,8},{12,10},{14,12},{16,14},{18,16},{20... | collective-permute-start | bytes 940040 | tf_op jit(solution)/shard_map/ppermute | solution.py:23
